TPU v7x, 32 devices: a whole 2x2x4 slice. The times are simulated.
32 devices in a mesh: district: 4 (over y, core), sub: 8 (over z, x).
Axes of the slice: x: 2, y: 2, z: 4, core: 2. Of those that a mesh axis runs over, the one named last changes fastest.
Arguments:
- cost_terms: bfloat16 [8, 512, 768], P('district', 'sub'), may hold values from -6 to 6
- neighbours: int32 [8, 512, 4], P('district', 'sub'), may hold values from 0 to 511, as said below
- relayout: int32 [8, 512], P('district'), may hold values from 0 to 511, as said below
- ownership: int32 [8, 512], P('district', 'sub'), may hold values from 0 to 31
- capacity: float32 [16, 48], replicated, may hold values from -67.88225 to 67.88225
- coupling: bfloat16 [8, 768, 192], P('district'), may hold values from -0.21875 to 0.21875
- solve_factor: bfloat16 [8, 768, 768], P('district')
Outputs:
- control_plan: float32 [8, 512, 768], P('district', 'sub')
- flow_prices: float32 [8, 512, 192], P('district', 'sub')
- reservoir_duals: float32 [16, 48], replicated
Inputs may be any that keep to these rules, and one draw needn't show every extreme that they name: `neighbours`: each entry lies within 16 of its own balanced position and differs from it. `relayout`: each row is a permutation; of the subsystems at geographic positions s * 64 to (s + 1) * 64 - 1, exactly 8 go to balanced positions j * 64 to (j + 1) * 64 - 1, for every s and j. `ownership`: values of 16 or more mean that the subsystem draws from no reservoir.
All inputs are finite; a program needn't handle non-finite values.
Results may differ from a plain program's by a relative error of at most 0.018.
Values may be sent and summed in bfloat16 or wider, within the bound.
No kernel may reach another device: no remote copies, remote signals or barrier semaphores. Data moves between devices by JAX's collectives and lax.ppermute only.
A program may use at most 64 MiB of HBM per device.

v0:
```python
import functools
import math

import jax
import jax.numpy as jnp
from jax import lax
from jax.experimental import pallas as pl
from jax.experimental.pallas import tpu as pltpu
from jax.sharding import PartitionSpec as P

REACH_SPAN = 16
LINK_COUNT = 4
RESERVOIRS = 16
OUTER_ITERS = 2
INNER_ITERS = 4

PRICE_STEP = 0.3
RESERVE_STEP = 1.0

LANES = 128
PAD = 2 * REACH_SPAN

BF = jnp.bfloat16
F32 = jnp.float32


def mm(a, b):
    return jnp.dot(a, b, preferred_element_type=F32)


def mm_nt(a, b):
    return lax.dot_general(a, b, (((1,), (1,)), ((), ())), preferred_element_type=F32)


def mm_tn(a, b):
    return lax.dot_general(a, b, (((0,), (0,)), ((), ())), preferred_element_type=F32)


def iota(shape, dim):
    return lax.broadcasted_iota(jnp.int32, shape, dim)


def each(count, step):
    if count <= 8:
        for i in range(count):
            step(i)
    else:
        lax.fori_loop(0, count, lambda i, c: (step(i), c)[1], 0)


def at(i, size):
    if isinstance(i, int):
        return pl.ds(i * size, size)
    return pl.ds(pl.multiple_of(i * size, size), size)


def window(i, size, width):
    if isinstance(i, int):
        return pl.ds(i * size, width)
    return pl.ds(pl.multiple_of(i * size, size), width)


def prepare_body(my_ref, cost_ref, s_ref, c_ref, nb_ref, own_ref, y_ref, z_ref, m_ref, pay_ref,
                 lhs, acc, *, rows, width, chunk, owner_at):
    d = pl.program_id(0)
    j = pl.program_id(1)

    @pl.when(j == 0)
    def _():
        lhs[:rows, :] = cost_ref[0]
        lhs[rows:, :] = c_ref[0].T
        acc[...] = jnp.zeros_like(acc)

    yz = mm(lhs[...], s_ref[0])
    y_ref[0] = yz[:rows]
    yzb = yz.astype(BF)
    z_ref[0] = yzb[rows:]
    acc[...] += mm(yzb, c_ref[0, pl.ds(pl.multiple_of(j * chunk, chunk), chunk), :])

    @pl.when(j == pl.num_programs(1) - 1)
    def _():
        pay_ref[0, :, 0:width] = (-acc[:rows]).astype(BF)
        m_ref[0] = acc[rows:].astype(BF)
        total = pay_ref.shape[2]
        own = own_ref[pl.ds(d, 1), :]
        slot = iota((total, rows), 0) - owner_at
        hot = ((slot == own) & (slot >= 0) & (slot < RESERVOIRS)).astype(F32)
        eye = (iota((rows, rows), 0) == iota((rows, rows), 1)).astype(F32)
        ext = mm_nt(eye.astype(BF), hot.astype(BF))
        off = (nb_ref[0] - my_ref[0] * rows - iota((rows, LINK_COUNT), 0)).astype(F32)
        lane = iota((rows, total), 1)
        for k in range(LINK_COUNT):
            ext = jnp.where(lane == width + k, off[:, k:k + 1], ext)
        pay_ref[0, :, width:] = ext[:, width:].astype(BF)


def band(off, rows, columns, shift, first_lane):
    column = iota((rows, columns), 1) - iota((rows, columns), 0) - shift
    out = (column == 0).astype(F32)
    for k in range(LINK_COUNT):
        offset = off[:, first_lane + k:first_lane + k + 1].astype(jnp.int32)
        out = out - jnp.where(column == offset, 1.0 / LINK_COUNT, 0.0)
    return out


def iterate_body(my_ref, g_ref, rel_ref, relown_ref, m_ref,
                 d0_ref, d1_ref, pb_ref, tb_ref, ql_ref, qg_ref, gm_ref, mp_ref,
                 off, dband, x, h, f0, t, exc, fl, *, rows, width, horizon, tile, owner_at):
    districts = g_ref.shape[1]
    subs = g_ref.shape[0]
    total = g_ref.shape[3]
    count = rows * subs
    blocks = count // tile
    low = total - LANES
    span = tile + 2 * PAD
    my = my_ref[0]
    half = iota((tile, LANES), 1)
    own_lane = owner_at - low

    def ext_of(v, power):
        moved = pltpu.roll(v, (power * RESERVOIRS - own_lane) % LANES, 1)
        keep = (half >= power * RESERVOIRS) & (half < (power + 1) * RESERVOIRS)
        return jnp.where(keep, moved, 0.0)

    for d in range(districts):
        off[d, :PAD, :] = jnp.zeros((PAD, LANES), F32)
        off[d, PAD + count:, :] = jnp.zeros((PAD, LANES), F32)
        x[d, :PAD, :] = jnp.zeros((PAD, total), BF)
        x[d, PAD + count:, :] = jnp.zeros((PAD, total), BF)
        exc[d, :PAD, :] = jnp.zeros((PAD, LANES), BF)
        exc[d, PAD + count:, :] = jnp.zeros((PAD, LANES), BF)

        def unpack(s):
            here = at(s, rows)
            if isinstance(s, int):
                padded = pl.ds(PAD + s * rows, rows)
            else:
                padded = pl.ds(pl.multiple_of(PAD + s * rows, PAD), rows)
            block = g_ref[s, d]
            t[d, here, :] = block[:, :width]
            off[d, padded, :] = block[:, low:].astype(F32)
            x[d, padded, :] = block

        each(subs, unpack)

        def order(i):
            place = iota((tile, count), 0) + i * tile
            hot = (place == rel_ref[d:d + 1, :]).astype(F32).astype(BF)
            f0[d, at(i, tile), :] = mm(hot, t[d])

        each(blocks, order)

        def bands(i):
            full = band(off[d, window(i, tile, span), :], span, span, 0, width - low).astype(BF)
            dband[d, at(i, tile), :] = mm(full[PAD:PAD + tile], full).astype(BF)
            if isinstance(i, int):
                padded = pl.ds(PAD + i * tile, tile)
            else:
                padded = pl.ds(pl.multiple_of(PAD + i * tile, PAD), tile)
            f = f0[d, at(i, tile), :]
            h[d, at(i, tile), :] = f
            x[d, padded, :width] = f.astype(BF)
            exc[d, padded, :] = ext_of(off[d, padded, :], 0).astype(BF)

        each(blocks, bands)

    steps = OUTER_ITERS * INNER_ITERS
    for k in range(1, steps):
        for d in range(districts):
            def spread(i):
                v = mm(dband[d, at(i, tile), :], x[d, window(i, tile, span), :])
                t[d, at(i, tile), :] = (PRICE_STEP * v[:, :width]).astype(BF)
                if k < INNER_ITERS:
                    if isinstance(i, int):
                        padded = pl.ds(PAD + i * tile, tile)
                    else:
                        padded = pl.ds(pl.multiple_of(PAD + i * tile, PAD), tile)
                    half_v = v[:, low:]
                    old = exc[d, padded, :].astype(F32)
                    exc[d, padded, :] = (old + ext_of(half_v, k)).astype(BF)
                    off[d, padded, :] = half_v

            each(blocks, spread)

        for d in range(districts):
            def advance(i):
                if isinstance(i, int):
                    padded = pl.ds(PAD + i * tile, tile)
                else:
                    padded = pl.ds(pl.multiple_of(PAD + i * tile, PAD), tile)
                f = f0[d, at(i, tile), :] - mm(t[d, at(i, tile), :], m_ref[d])
                new = h[d, at(i, tile), :] + f
                h[d, at(i, tile), :] = new
                x[d, padded, :width] = new.astype(BF)
                if k < INNER_ITERS - 1:
                    x[d, padded, width:] = off[d, padded, :][:, width - low:].astype(BF)
                if k == INNER_ITERS - 1 or k == steps - 1:
                    fl[d, at(i, tile), :] = f.astype(BF)

            each(blocks, advance)

        if k == INNER_ITERS - 1 or k == steps - 1:
            target = d0_ref if k == INNER_ITERS - 1 else d1_ref
            draws = jnp.zeros((RESERVOIRS, LANES), F32)
            for d in range(districts):
                draws += mm_tn(exc[d, PAD:PAD + count, :], fl[d, :, :LANES])[:RESERVOIRS]
            target[...] = draws

    per = LANES // rows
    for d in range(districts):
        own_rel = relown_ref[d:d + 1, 0:rows]
        for q in range(1, per):
            own_rel = jnp.where(my % per == q, relown_ref[d:d + 1, q * rows:(q + 1) * rows], own_rel)
        hot = (iota((count, rows), 0) == own_rel).astype(F32).astype(BF)
        tb_ref[d] = mm_tn(hot, t[d])
        qg_ref[d] = mm_tn(hot, exc[d, PAD:PAD + count, :]).astype(BF)
        start = pl.multiple_of(my * rows, rows)
        own_off = (g_ref[my, d])[:, low:].astype(F32)
        own_band = band(own_off, rows, rows + 2 * PAD, PAD, width - low).astype(BF)
        pb_ref[d] = PRICE_STEP * mm(own_band, x[d, pl.ds(start, rows + 2 * PAD), :])[:, :width]
        ql_ref[d] = mm(own_band, exc[d, pl.ds(start, rows + 2 * PAD), :]).astype(BF)
        gm_ref[d] = mm_tn(exc[d, PAD:PAD + count, :], exc[d, PAD:PAD + count, :])[:RESERVOIRS].astype(BF)
        power = (iota((horizon, width), 0) == iota((horizon, width), 1)).astype(F32).astype(BF)
        mp_ref[d, 0] = power
        for j in range(INNER_ITERS):
            power = mm(power, m_ref[d]).astype(BF)
            mp_ref[d, j + 1] = power


def finish_body(dr_ref, cap_ref, d1_ref, pb_ref, tb_ref, ql_ref, qg_ref, gm_ref, mp_ref, y_ref, z_ref,
                plan_ref, price_ref, dual_ref, draw_ref, *, scale, horizon):
    districts = pb_ref.shape[0]
    drawn = dr_ref[0]
    for q in range(1, dr_ref.shape[0]):
        drawn = drawn + dr_ref[q]
    duals = (drawn[:, :horizon] - cap_ref[...]) * scale
    dual_ref[...] = duals
    high = duals.astype(BF)
    both = jnp.concatenate([duals, duals - high.astype(F32)], axis=0).astype(BF)
    n = INNER_ITERS
    draws = d1_ref[...]
    for d in range(districts):
        grown = []
        for j in range(n + 1):
            parts = mm(both, mp_ref[d, j])
            grown.append(parts[:RESERVOIRS] + parts[RESERVOIRS:])

        def stacked(first, weights):
            rows = [w * grown[first + j] for j, w in enumerate(weights)]
            filler = jnp.zeros((LANES - n * RESERVOIRS, rows[0].shape[1]), F32)
            whole = jnp.concatenate(rows + [filler], axis=0)
            top = whole.astype(BF)
            return top, (whole - top.astype(F32)).astype(BF)

        def apply(left, pair):
            return mm(left, pair[0]) + mm(left, pair[1])

        term = [math.comb(n - 1, j) * (-PRICE_STEP) ** j for j in range(n)]
        sums = [-PRICE_STEP * math.comb(n, j + 1) * (-PRICE_STEP) ** j for j in range(n)]
        prices = (tb_ref[d] + apply(qg_ref[d], stacked(0, term))).astype(BF)
        plan_ref[d] = -(y_ref[d] + mm(prices, z_ref[d]))
        price_ref[d] = pb_ref[d] + apply(ql_ref[d], stacked(1, sums))
        draws = draws - apply(gm_ref[d], stacked(1, term))[:, :LANES]
    draw_ref[...] = draws


def on_device(cost_terms, neighbours, relayout, ownership, capacity, coupling, solve_factor):
    districts, rows, unknowns = cost_terms.shape
    width = coupling.shape[2]
    horizon = capacity.shape[1]
    subs = lax.axis_size("sub")
    count = rows * subs
    assert relayout.shape[1] == count
    my = lax.axis_index("sub").astype(jnp.int32).reshape(1)
    chunk = 256
    chunks = unknowns // chunk
    total = width + 64
    owner_at = width + 16
    tile = LANES
    load_count = districts * lax.axis_size("district") * count // (2 * RESERVOIRS)
    scale = RESERVE_STEP / math.sqrt(load_count)
    limit = pltpu.CompilerParams(vmem_limit_bytes=56 * 1024 * 1024)

    y, z, m, payload = pl.pallas_call(
        functools.partial(prepare_body, rows=rows, width=width, chunk=chunk, owner_at=owner_at),
        grid_spec=pltpu.PrefetchScalarGridSpec(
            num_scalar_prefetch=1,
            grid=(districts, chunks),
            in_specs=[
                pl.BlockSpec((1, rows, unknowns), lambda d, j, s: (d, 0, 0)),
                pl.BlockSpec((1, unknowns, chunk), lambda d, j, s: (d, 0, j)),
                pl.BlockSpec((1, unknowns, width), lambda d, j, s: (d, 0, 0)),
                pl.BlockSpec((1, rows, LINK_COUNT), lambda d, j, s: (d, 0, 0)),
                pl.BlockSpec((districts, rows), lambda d, j, s: (0, 0)),
            ],
            out_specs=[
                pl.BlockSpec((1, rows, chunk), lambda d, j, s: (d, 0, j)),
                pl.BlockSpec((1, width, chunk), lambda d, j, s: (d, 0, j)),
                pl.BlockSpec((1, width, width), lambda d, j, s: (d, 0, 0)),
                pl.BlockSpec((1, rows, total), lambda d, j, s: (d, 0, 0)),
            ],
            scratch_shapes=[
                pltpu.VMEM((rows + width, unknowns), BF),
                pltpu.VMEM((rows + width, width), F32),
            ],
        ),
        out_shape=[
            jax.ShapeDtypeStruct((districts, rows, unknowns), F32),
            jax.ShapeDtypeStruct((districts, width, unknowns), BF),
            jax.ShapeDtypeStruct((districts, width, width), BF),
            jax.ShapeDtypeStruct((districts, rows, total), BF),
        ],
        compiler_params=limit,
        name="prepare",
    )(my, cost_terms, solve_factor, coupling, neighbours, ownership)

    gathered = lax.all_gather(payload, "sub", axis=0, tiled=False)

    whole = lambda shape: pl.BlockSpec(shape, lambda i, s: (0,) * len(shape))
    per = LANES // rows
    out_shapes = [
        ((RESERVOIRS, LANES), F32),
        ((RESERVOIRS, LANES), F32),
        ((districts, rows, width), F32),
        ((districts, rows, width), F32),
        ((districts, rows, LANES), BF),
        ((districts, rows, LANES), BF),
        ((districts, RESERVOIRS, LANES), BF),
        ((districts, INNER_ITERS + 1, horizon, width), BF),
    ]
    d0, d1, pb, tb, ql, qg, gm, mp = pl.pallas_call(
        functools.partial(
            iterate_body, rows=rows, width=width, horizon=horizon, tile=tile, owner_at=owner_at
        ),
        grid_spec=pltpu.PrefetchScalarGridSpec(
            num_scalar_prefetch=1,
            grid=(1,),
            in_specs=[
                whole((subs, districts, rows, total)),
                whole((districts, count)),
                pl.BlockSpec((districts, LANES), lambda i, s: (0, s[0] // per)),
                whole((districts, width, width)),
            ],
            out_specs=[whole(shape) for shape, _ in out_shapes],
            scratch_shapes=[
                pltpu.VMEM((districts, count + 2 * PAD, LANES), F32),
                pltpu.VMEM((districts, count, tile + 2 * PAD), BF),
                pltpu.VMEM((districts, count + 2 * PAD, total), BF),
                pltpu.VMEM((districts, count, width), F32),
                pltpu.VMEM((districts, count, width), F32),
                pltpu.VMEM((districts, count, width), BF),
                pltpu.VMEM((districts, count + 2 * PAD, LANES), BF),
                pltpu.VMEM((districts, count, width), BF),
            ],
        ),
        out_shape=[jax.ShapeDtypeStruct(shape, kind) for shape, kind in out_shapes],
        compiler_params=limit,
        name="iterate",
    )(my, gathered, relayout, relayout, m)

    drawn = lax.all_gather(d0, "district", axis=0, tiled=False)

    plan, prices, duals, draws = pl.pallas_call(
        functools.partial(finish_body, scale=scale, horizon=horizon),
        out_shape=[
            jax.ShapeDtypeStruct((districts, rows, unknowns), F32),
            jax.ShapeDtypeStruct((districts, rows, width), F32),
            jax.ShapeDtypeStruct((RESERVOIRS, horizon), F32),
            jax.ShapeDtypeStruct((RESERVOIRS, LANES), F32),
        ],
        compiler_params=limit,
        name="finish",
    )(drawn, capacity, d1, pb, tb, ql, qg, gm, mp, y, z)

    drawn = lax.all_gather(draws, "district", axis=0, tiled=False)
    total_draws = jnp.sum(drawn, axis=0)[:, :horizon]
    duals = duals + (total_draws - capacity) * scale
    return plan, prices, duals


def solution(mesh):
    placed = (
        P("district", "sub", None),
        P("district", "sub", None),
        P("district", None),
        P("district", "sub"),
        P(),
        P("district", None, None),
        P("district", None, None),
    )
    return jax.shard_map(
        on_device,
        mesh=mesh,
        in_specs=placed,
        out_specs=(P("district", "sub", None), P("district", "sub", None), P()),
        check_vma=False,
    )
```

profile of v0, /device:TPU:0, one launch (start us, length us, event | category | flops | bytes accessed | tf_op | source)
XLA Modules:
  0.0 70.1 jit_solution(8307938905658315276)
XLA Ops:
  0.6 1.4 %copy.13.nb_ref = s32[2,64,4]{2,1,0:T(8,128)} copy(s32[2,64,4]{1,2,0:T(4,128)} %param.8) | data formatting | bytes 4096 | tf_op args[1]
  2.1 2.2 %copy.12.c_ref = bf16[2,768,192]{2,1,0:T(8,128)(2,1)} copy(bf16[2,768,192]{1,2,0:T(8,128)(2,1)} %param.12) | data formatting | bytes 1179648 | tf_op args[5]
  4.3 6.6 %prepare.1 = (f32[2,64,768]{2,1,0:T(8,128)}, bf16[2,192,768]{2,1,0:T(8,128)(2,1)}, bf16[2,192,192]{2,1,0:T(8,128)(2,1)}, bf16[2,64,256]{2,1,0:T(8,128)(2,1)}) custom-call(s32[1]{0:T(128)} %bitcast.my_ref, bf16[2,64,768]{2,1,0:T(8,128)(2,1)} %cost_ref.1, bf16[2,768,768]{2,1,0:T(8,128)(2,1)} %s_ref.1, bf16[2,768,192]{2,1,0:T(8,128)(2,1)} %copy.12.c_ref, ...), custom_call_target="tpu_custom_call" | custom-call | tf_op jit(solution)/shard_map/prepare/pallas_call | solution.py:284
  10.9 0.0 copy-start
  10.9 35.4 %all-gather = bf16[16,64,256]{2,1,0:T(8,128)(2,1)} all-gather(bf16[2,64,256]{2,1,0:T(8,128)(2,1)} %get-tuple-element.19), channel_id=2, replica_groups=mesh['district'=4,'sub'=8] {'sub'}, dimensions={0}, use_global_device_ids=true | all-gather | bytes 589824 | tf_op jit(solution)/shard_map/all_gather | solution.py:317
  46.3 7.4 %iterate.1 = (f32[16,128]{1,0:T(8,128)}, f32[16,128]{1,0:T(8,128)}, f32[2,64,192]{2,1,0:T(8,128)}, f32[2,64,192]{2,1,0:T(8,128)}, bf16[2,64,128]{2,1,0:T(8,128)(...) custom-call(s32[1]{0:T(128)} %bitcast.my_ref, ...), custom_call_target="tpu_custom_call" | custom-call | tf_op jit(solution)/shard_map/iterate/pallas_call | solution.py:331
  53.7 6.6 %all-gather.1 = f32[64,128]{1,0:T(8,128)} all-gather(f32[16,128]{1,0:T(8,128)} %get-tuple-element.21), channel_id=3, replica_groups=mesh['district'=4,'sub'=8] {'district'}, dimensions={0}, use_global_device_ids=true | all-gather | bytes 40960 | tf_op jit(solution)/shard_map/all_gather | solution.py:361
  60.4 3.1 %finish.1 = (f32[2,64,768]{2,1,0:T(8,128)}, f32[2,64,192]{2,1,0:T(8,128)}, f32[16,48]{1,0:T(8,128)}, f32[16,128]{1,0:T(8,128)}) custom-call(f32[4,16,128]{2,1,0:T(8,128)} %bitcast.5, f32[16,48]{1,0:T(8,128)} %cap_ref.1, f32[16,128]{1,0:T(8,128)} %get-tuple-element.22.d1_ref, f32[2,64,192]{2,1,0:T(8,128)} %get-tuple-element.23.pb_ref, ...), custom_call_target="tpu_custom_call" | custom-call | tf_op jit(solution)/shard_map/finish/pallas_call | solution.py:363
  63.4 5.4 %all-gather.2 = f32[64,128]{1,0:T(8,128)S(1)} all-gather(f32[16,128]{1,0:T(8,128)} %get-tuple-element.34), channel_id=4, replica_groups=mesh['district'=4,'sub'=8] {'district'}, dimensions={0}, use_global_device_ids=true | all-gather | bytes 40960 | tf_op jit(solution)/shard_map/all_gather | solution.py:375
  68.8 0.0 copy-done
  68.8 1.3 %fusion.1 = f32[16,48]{1,0:T(8,128)} fusion(f32[16,48]{1,0:T(8,128)} %get-tuple-element.33, f32[16,48]{1,0:T(8,128)S(1)} %copy-done, f32[16,128]{1,0:T(8,128)S(1)} %reduce_sum.9), kind=kLoop, calls=%fused_computation.2 | loop fusion | flops 2304 | bytes 12288 | tf_op jit(solution)/shard_map/add | solution.py:377
  (1 shorter events, 0.0 us)
Async XLA Ops:
  10.9 58.0 %copy-start = (f32[16,48]{1,0:T(8,128)S(1)}, f32[16,48]{1,0:T(8,128)}, u32[]{:S(2)}) copy-start(f32[16,48]{1,0:T(8,128)} %cap_ref.1) | copy-start | bytes 9220
where the time goes:
time: 70.6 us; the launch traced here: 70.1 us
  blocking collectives  47.4 us (67%)
  Pallas kernels  17.1 us (24%)
  local copies, waits for them, and re-layouts  3.64 us (5%)
  other arithmetic  1.31 us (2%)
    all_gather x1, blocking collectives, on_device(): gathered = lax.all_gather(payload, 'sub', axis=0, tiled=False)  35.4 us
    pallas_call x1, Pallas kernels, on_device(): pl.pallas_call(functools.partial(iterate_body, rows=rows, width=width, ho...  7.43 us
    all_gather x1, blocking collectives, on_device(): drawn = lax.all_gather(d0, 'district', axis=0, tiled=False)  6.61 us
    pallas_call x1, Pallas kernels, on_device(): pl.pallas_call(functools.partial(prepare_body, rows=rows, width=width, ch...  6.58 us
    all_gather x1, blocking collectives, on_device(): drawn = lax.all_gather(draws, 'district', axis=0, tiled=False)  5.38 us
    unnamed x4, local copies, waits for them, and re-layouts  3.64 us
    pallas_call x1, Pallas kernels, on_device(): pl.pallas_call(functools.partial(finish_body, scale=scale, horizon=horizo...  3.08 us

commit v1 on v0

--- a/solution.py
+++ b/solution.py
@@ -60,6 +60,44 @@
     return pl.ds(pl.multiple_of(i * size, size), width)
 
 
+def gather_blocks(block, axis):
+    n = lax.axis_size(axis)
+    if n > 8 or n % 2:
+        return [lax.all_gather(block, axis, axis=0, tiled=False)]
+    other = lax.ppermute(block, axis, [(i, i ^ 1) for i in range(n)])
+    pair = jnp.stack([block, other])
+    turned = [
+        lax.ppermute(pair, axis, [(i, (i + 2 * k) % n) for i in range(n)]) for k in range(1, n // 2)
+    ]
+    return [pair] + turned
+
+
+def origins(my, n, arrays):
+    if arrays == 1:
+        return [[s for s in range(n)]]
+    out = []
+    for k in range(arrays):
+        source = lax.rem(my + n - 2 * k, n)
+        swapped = source + 1 - 2 * lax.rem(source, 2)
+        out.append([source, swapped])
+    return out
+
+
+def gather_few(block, axis):
+    n = lax.axis_size(axis)
+    if n & (n - 1):
+        whole = lax.all_gather(block, axis, axis=0, tiled=False)
+        return [whole[i] for i in range(n)]
+    return [block] + [lax.ppermute(block, axis, [(i, i ^ k) for i in range(n)]) for k in range(1, n)]
+
+
+def tree(parts):
+    while len(parts) > 1:
+        last = [parts[-1]] if len(parts) % 2 else []
+        parts = [parts[i] + parts[i + 1] for i in range(0, len(parts) - 1, 2)] + last
+    return parts[0]
+
+
 def prepare_body(my_ref, cost_ref, s_ref, c_ref, nb_ref, own_ref, y_ref, z_ref, m_ref, pay_ref,
                  lhs, acc, *, rows, width, chunk, owner_at):
     d = pl.program_id(0)
@@ -68,14 +106,14 @@
     @pl.when(j == 0)
     def _():
         lhs[:rows, :] = cost_ref[0]
-        lhs[rows:, :] = c_ref[0].T
+        lhs[rows:, :] = c_ref[0]
         acc[...] = jnp.zeros_like(acc)
 
     yz = mm(lhs[...], s_ref[0])
     y_ref[0] = yz[:rows]
     yzb = yz.astype(BF)
     z_ref[0] = yzb[rows:]
-    acc[...] += mm(yzb, c_ref[0, pl.ds(pl.multiple_of(j * chunk, chunk), chunk), :])
+    acc[...] += mm_nt(yzb, c_ref[0, :, pl.ds(pl.multiple_of(j * chunk, chunk), chunk)])
 
     @pl.when(j == pl.num_programs(1) - 1)
     def _():
@@ -86,11 +124,11 @@
         slot = iota((total, rows), 0) - owner_at
         hot = ((slot == own) & (slot >= 0) & (slot < RESERVOIRS)).astype(F32)
         eye = (iota((rows, rows), 0) == iota((rows, rows), 1)).astype(F32)
+        off = (nb_ref[0] - my_ref[0] * rows - iota((LINK_COUNT, rows), 1)).astype(F32)
+        line = iota((total, rows), 0)
+        for k in range(LINK_COUNT):
+            hot = jnp.where(line == width + k, off[k:k + 1, :], hot)
         ext = mm_nt(eye.astype(BF), hot.astype(BF))
-        off = (nb_ref[0] - my_ref[0] * rows - iota((rows, LINK_COUNT), 0)).astype(F32)
-        lane = iota((rows, total), 1)
-        for k in range(LINK_COUNT):
-            ext = jnp.where(lane == width + k, off[:, k:k + 1], ext)
         pay_ref[0, :, width:] = ext[:, width:].astype(BF)
 
 
@@ -103,12 +141,13 @@
     return out
 
 
-def iterate_body(my_ref, g_ref, rel_ref, relown_ref, m_ref,
-                 d0_ref, d1_ref, pb_ref, tb_ref, ql_ref, qg_ref, gm_ref, mp_ref,
-                 off, dband, x, h, f0, t, exc, fl, *, rows, width, horizon, tile, owner_at):
-    districts = g_ref.shape[1]
-    subs = g_ref.shape[0]
-    total = g_ref.shape[3]
+def iterate_body(my_ref, *refs, arrays, subs, rows, width, horizon, tile, owner_at):
+    g_refs = refs[:arrays]
+    rel_ref, relown_ref, m_ref = refs[arrays:arrays + 3]
+    msg_ref, pb_ref, tb_ref, ql_ref, qg_ref, mp_ref = refs[arrays + 3:arrays + 9]
+    off, dband, x, h, f0, t, exc, fl = refs[arrays + 9:]
+    districts = g_refs[0].shape[1]
+    total = g_refs[0].shape[3]
     count = rows * subs
     blocks = count // tile
     low = total - LANES
@@ -130,18 +169,22 @@
         exc[d, :PAD, :] = jnp.zeros((PAD, LANES), BF)
         exc[d, PAD + count:, :] = jnp.zeros((PAD, LANES), BF)
 
-        def unpack(s):
+        def unpack(s, block):
             here = at(s, rows)
             if isinstance(s, int):
                 padded = pl.ds(PAD + s * rows, rows)
             else:
                 padded = pl.ds(pl.multiple_of(PAD + s * rows, PAD), rows)
-            block = g_ref[s, d]
             t[d, here, :] = block[:, :width]
             off[d, padded, :] = block[:, low:].astype(F32)
             x[d, padded, :] = block
 
-        each(subs, unpack)
+        if arrays == 1:
+            each(subs, lambda s: unpack(s, g_refs[0][s, d]))
+        else:
+            for g_ref, sources in zip(g_refs, origins(my, subs, arrays)):
+                for b, s in enumerate(sources):
+                    unpack(s, g_ref[b, d])
 
         def order(i):
             place = iota((tile, count), 0) + i * tile
@@ -200,11 +243,13 @@
             each(blocks, advance)
 
         if k == INNER_ITERS - 1 or k == steps - 1:
-            target = d0_ref if k == INNER_ITERS - 1 else d1_ref
+            first = 0 if k == INNER_ITERS - 1 else 2 * RESERVOIRS
             draws = jnp.zeros((RESERVOIRS, LANES), F32)
             for d in range(districts):
                 draws += mm_tn(exc[d, PAD:PAD + count, :], fl[d, :, :LANES])[:RESERVOIRS]
-            target[...] = draws
+            top = draws.astype(BF)
+            msg_ref[first:first + RESERVOIRS, :] = top
+            msg_ref[first + RESERVOIRS:first + 2 * RESERVOIRS, :] = (draws - top.astype(F32)).astype(BF)
 
     per = LANES // rows
     for d in range(districts):
@@ -215,53 +260,71 @@
         tb_ref[d] = mm_tn(hot, t[d])
         qg_ref[d] = mm_tn(hot, exc[d, PAD:PAD + count, :]).astype(BF)
         start = pl.multiple_of(my * rows, rows)
-        own_off = (g_ref[my, d])[:, low:].astype(F32)
+        own_off = (g_refs[0][my if arrays == 1 else 0, d])[:, low:].astype(F32)
         own_band = band(own_off, rows, rows + 2 * PAD, PAD, width - low).astype(BF)
         pb_ref[d] = PRICE_STEP * mm(own_band, x[d, pl.ds(start, rows + 2 * PAD), :])[:, :width]
         ql_ref[d] = mm(own_band, exc[d, pl.ds(start, rows + 2 * PAD), :]).astype(BF)
-        gm_ref[d] = mm_tn(exc[d, PAD:PAD + count, :], exc[d, PAD:PAD + count, :])[:RESERVOIRS].astype(BF)
+        start = 4 * RESERVOIRS + d * (RESERVOIRS + INNER_ITERS * horizon)
+        response = mm_tn(exc[d, PAD:PAD + count, :], exc[d, PAD:PAD + count, :])[:RESERVOIRS]
+        msg_ref[start:start + RESERVOIRS, :] = response.astype(BF)
+        start += RESERVOIRS
         power = (iota((horizon, width), 0) == iota((horizon, width), 1)).astype(F32).astype(BF)
         mp_ref[d, 0] = power
         for j in range(INNER_ITERS):
             power = mm(power, m_ref[d]).astype(BF)
             mp_ref[d, j + 1] = power
-
-
-def finish_body(dr_ref, cap_ref, d1_ref, pb_ref, tb_ref, ql_ref, qg_ref, gm_ref, mp_ref, y_ref, z_ref,
-                plan_ref, price_ref, dual_ref, draw_ref, *, scale, horizon):
+            msg_ref[start + j * horizon:start + (j + 1) * horizon, :] = power[:, :LANES]
+
+
+def finish_body(*refs, pieces, scale, horizon):
+    msgs = refs[:pieces]
+    cap_ref, pb_ref, tb_ref, ql_ref, qg_ref, mp_ref, y_ref, z_ref = refs[pieces:pieces + 8]
+    plan_ref, price_ref, dual_ref = refs[pieces + 8:]
     districts = pb_ref.shape[0]
-    drawn = dr_ref[0]
-    for q in range(1, dr_ref.shape[0]):
-        drawn = drawn + dr_ref[q]
-    duals = (drawn[:, :horizon] - cap_ref[...]) * scale
-    dual_ref[...] = duals
+    n = INNER_ITERS
+
+    def drawn(first):
+        sums = []
+        for msg in msgs:
+            high = msg[first:first + RESERVOIRS, :].astype(F32)
+            sums.append(high + msg[first + RESERVOIRS:first + 2 * RESERVOIRS, :].astype(F32))
+        return sums
+
+    duals = (tree(drawn(0))[:, :horizon] - cap_ref[...]) * scale
     high = duals.astype(BF)
     both = jnp.concatenate([duals, duals - high.astype(F32)], axis=0).astype(BF)
-    n = INNER_ITERS
-    draws = d1_ref[...]
+    term = [math.comb(n - 1, j) * (-PRICE_STEP) ** j for j in range(n)]
+    sums = [-PRICE_STEP * math.comb(n, j + 1) * (-PRICE_STEP) ** j for j in range(n)]
+
+    def grow(power):
+        parts = mm(both, power)
+        return parts[:RESERVOIRS] + parts[RESERVOIRS:]
+
+    def stacked(grown, weights):
+        rows = [w * g for g, w in zip(grown, weights)]
+        filler = jnp.zeros((LANES - n * RESERVOIRS, rows[0].shape[1]), F32)
+        return jnp.concatenate(rows + [filler], axis=0)
+
+    def apply(left, whole):
+        top = whole.astype(BF)
+        return mm(left, top) + mm(left, (whole - top.astype(F32)).astype(BF))
+
     for d in range(districts):
-        grown = []
-        for j in range(n + 1):
-            parts = mm(both, mp_ref[d, j])
-            grown.append(parts[:RESERVOIRS] + parts[RESERVOIRS:])
-
-        def stacked(first, weights):
-            rows = [w * grown[first + j] for j, w in enumerate(weights)]
-            filler = jnp.zeros((LANES - n * RESERVOIRS, rows[0].shape[1]), F32)
-            whole = jnp.concatenate(rows + [filler], axis=0)
-            top = whole.astype(BF)
-            return top, (whole - top.astype(F32)).astype(BF)
-
-        def apply(left, pair):
-            return mm(left, pair[0]) + mm(left, pair[1])
-
-        term = [math.comb(n - 1, j) * (-PRICE_STEP) ** j for j in range(n)]
-        sums = [-PRICE_STEP * math.comb(n, j + 1) * (-PRICE_STEP) ** j for j in range(n)]
-        prices = (tb_ref[d] + apply(qg_ref[d], stacked(0, term))).astype(BF)
+        grown = [grow(mp_ref[d, j]) for j in range(n + 1)]
+        prices = (tb_ref[d] + apply(qg_ref[d], stacked(grown, term))).astype(BF)
         plan_ref[d] = -(y_ref[d] + mm(prices, z_ref[d]))
-        price_ref[d] = pb_ref[d] + apply(ql_ref[d], stacked(1, sums))
-        draws = draws - apply(gm_ref[d], stacked(1, term))[:, :LANES]
-    draw_ref[...] = draws
+        price_ref[d] = pb_ref[d] + apply(ql_ref[d], stacked(grown[1:], sums))
+
+    draws = []
+    for msg, value in zip(msgs, drawn(2 * RESERVOIRS)):
+        for d in range(districts):
+            start = 4 * RESERVOIRS + d * (RESERVOIRS + n * horizon)
+            response = msg[start:start + RESERVOIRS, :]
+            start += RESERVOIRS
+            grown = [grow(msg[start + j * horizon:start + (j + 1) * horizon, :]) for j in range(n)]
+            value = value - apply(response, stacked(grown, term))
+        draws.append(value)
+    dual_ref[...] = duals + (tree(draws)[:, :horizon] - cap_ref[...]) * scale
 
 
 def on_device(cost_terms, neighbours, relayout, ownership, capacity, coupling, solve_factor):
@@ -289,8 +352,8 @@
             in_specs=[
                 pl.BlockSpec((1, rows, unknowns), lambda d, j, s: (d, 0, 0)),
                 pl.BlockSpec((1, unknowns, chunk), lambda d, j, s: (d, 0, j)),
-                pl.BlockSpec((1, unknowns, width), lambda d, j, s: (d, 0, 0)),
-                pl.BlockSpec((1, rows, LINK_COUNT), lambda d, j, s: (d, 0, 0)),
+                pl.BlockSpec((1, width, unknowns), lambda d, j, s: (d, 0, 0)),
+                pl.BlockSpec((1, LINK_COUNT, rows), lambda d, j, s: (d, 0, 0)),
                 pl.BlockSpec((districts, rows), lambda d, j, s: (0, 0)),
             ],
             out_specs=[
@@ -312,31 +375,30 @@
         ],
         compiler_params=limit,
         name="prepare",
-    )(my, cost_terms, solve_factor, coupling, neighbours, ownership)
-
-    gathered = lax.all_gather(payload, "sub", axis=0, tiled=False)
+    )(my, cost_terms, solve_factor, coupling.swapaxes(1, 2), neighbours.swapaxes(1, 2), ownership)
+
+    gathered = gather_blocks(payload, "sub")
 
     whole = lambda shape: pl.BlockSpec(shape, lambda i, s: (0,) * len(shape))
     per = LANES // rows
+    message = 4 * RESERVOIRS + districts * (RESERVOIRS + INNER_ITERS * horizon)
     out_shapes = [
-        ((RESERVOIRS, LANES), F32),
-        ((RESERVOIRS, LANES), F32),
+        ((message, LANES), BF),
         ((districts, rows, width), F32),
         ((districts, rows, width), F32),
         ((districts, rows, LANES), BF),
         ((districts, rows, LANES), BF),
-        ((districts, RESERVOIRS, LANES), BF),
         ((districts, INNER_ITERS + 1, horizon, width), BF),
     ]
-    d0, d1, pb, tb, ql, qg, gm, mp = pl.pallas_call(
+    sent, pb, tb, ql, qg, mp = pl.pallas_call(
         functools.partial(
-            iterate_body, rows=rows, width=width, horizon=horizon, tile=tile, owner_at=owner_at
+            iterate_body, arrays=len(gathered), subs=subs, rows=rows, width=width, horizon=horizon, tile=tile, owner_at=owner_at
         ),
         grid_spec=pltpu.PrefetchScalarGridSpec(
             num_scalar_prefetch=1,
             grid=(1,),
             in_specs=[
-                whole((subs, districts, rows, total)),
+                *[whole(piece.shape) for piece in gathered],
                 whole((districts, count)),
                 pl.BlockSpec((districts, LANES), lambda i, s: (0, s[0] // per)),
                 whole((districts, width, width)),
@@ -356,25 +418,20 @@
         out_shape=[jax.ShapeDtypeStruct(shape, kind) for shape, kind in out_shapes],
         compiler_params=limit,
         name="iterate",
-    )(my, gathered, relayout, relayout, m)
-
-    drawn = lax.all_gather(d0, "district", axis=0, tiled=False)
-
-    plan, prices, duals, draws = pl.pallas_call(
-        functools.partial(finish_body, scale=scale, horizon=horizon),
+    )(my, *gathered, relayout, relayout, m)
+
+    received = gather_few(sent, "district")
+
+    plan, prices, duals = pl.pallas_call(
+        functools.partial(finish_body, pieces=len(received), scale=scale, horizon=horizon),
         out_shape=[
             jax.ShapeDtypeStruct((districts, rows, unknowns), F32),
             jax.ShapeDtypeStruct((districts, rows, width), F32),
             jax.ShapeDtypeStruct((RESERVOIRS, horizon), F32),
-            jax.ShapeDtypeStruct((RESERVOIRS, LANES), F32),
         ],
         compiler_params=limit,
         name="finish",
-    )(drawn, capacity, d1, pb, tb, ql, qg, gm, mp, y, z)
-
-    drawn = lax.all_gather(draws, "district", axis=0, tiled=False)
-    total_draws = jnp.sum(drawn, axis=0)[:, :horizon]
-    duals = duals + (total_draws - capacity) * scale
+    )(*received, capacity, pb, tb, ql, qg, mp, y, z)
     return plan, prices, duals
 
 

time: 70.6 us -> 49.7 us (0.70)
  blocking collectives: 47.4 us -> 0 us
  waiting for transfers between devices: 0 us -> 18.8 us
  starting transfers between devices: 0 us -> 10.1 us
  local copies, waits for them, and re-layouts: 3.64 us -> 1.37 us
    all_gather x3 -> x0, blocking collectives: 47.4 us -> none  [the longest x1 35.4 us: on_device(): gathered = lax.all_gather(payload, 'sub', axis=0, tiled=False)]
    ppermute x0 -> x7, waiting for transfers between devices: none -> 18.8 us  [the longest x3 9.79 us: gather_blocks(): lax.ppermute(pair, axis, [(i, (i + 2 * k) % n) for i in range(n)])]
    ppermute x0 -> x7, starting transfers between devices: none -> 10.1 us  [the longest x3 5.2 us: gather_blocks(): lax.ppermute(pair, axis, [(i, (i + 2 * k) % n) for i in range(n)])]
    unnamed x4 -> x14, local copies, waits for them, and re-layouts: 3.64 us -> 1.37 us
    add x1 -> x0, other arithmetic: 1.3 us -> none  [on_device(): duals = duals + (total_draws - capacity) * scale]
    another operation x0 -> x1, other arithmetic: none -> 0.85 us  [gather_blocks(): pair = jnp.stack([block, other])]
  transfers between devices with their start and end apart: 0 -> 7, of which waited for: 0 -> 5; matrix products, arithmetic and copies ran while one was open for 0% -> 0% of each run, Pallas kernels for 0% -> 0%
where the time goes in v1:
time: 49.7 us; the launch traced here: 49.3 us
  waiting for transfers between devices  18.8 us (38%)
  Pallas kernels  17.5 us (35%)
  starting transfers between devices  10.1 us (20%)
  local copies, waits for them, and re-layouts  1.37 us (3%)
  other arithmetic  0.85 us (2%)
  between operations  0.68 us (1%)
    ppermute x3, waiting for transfers between devices, gather_blocks(): lax.ppermute(pair, axis, [(i, (i + 2 * k) % n) for i in range(n)])  9.79 us
    pallas_call x1, Pallas kernels, on_device(): pl.pallas_call(functools.partial(iterate_body, arrays=len(gathered), subs...  7.79 us
    ppermute x3, waiting for transfers between devices, gather_few(): lax.ppermute(block, axis, [(i, i ^ k) for i in range(n)])  6.6 us
    pallas_call x1, Pallas kernels, on_device(): pl.pallas_call(functools.partial(prepare_body, rows=rows, width=width, ch...  6.32 us
    ppermute x3, starting transfers between devices, gather_blocks(): lax.ppermute(pair, axis, [(i, (i + 2 * k) % n) for i in range(n)])  5.2 us
    pallas_call x1, Pallas kernels, on_device(): pl.pallas_call(functools.partial(finish_body, pieces=len(received), scale...  3.39 us
    ppermute x1, starting transfers between devices, gather_blocks(): other = lax.ppermute(block, axis, [(i, i ^ 1) for i in range(n)])  3.03 us
    ppermute x1, waiting for transfers between devices, gather_blocks(): other = lax.ppermute(block, axis, [(i, i ^ 1) for i in range(n)])  2.46 us
  transfers between devices with their start and end apart: 7, of which 5 were waited for; matrix products, arithmetic and copies ran while one was open for 0% of the time, Pallas kernels for 0%

profile of v1, /device:TPU:0, one launch (start us, length us, event | category | flops | bytes accessed | tf_op | source)
XLA Modules:
  0.0 49.3 jit_solution(8019275521267964833)
XLA Ops:
  0.6 6.3 %prepare.1 = (f32[2,64,768]{2,1,0:T(8,128)}, bf16[2,192,768]{2,1,0:T(8,128)(2,1)}, bf16[2,192,192]{2,1,0:T(8,128)(2,1)}, bf16[2,64,256]{2,1,0:T(8,128)(2,1)}) custom-call(s32[1]{0:T(128)} %bitcast.my_ref, bf16[2,64,768]{2,1,0:T(8,128)(2,1)} %cost_ref.1, bf16[2,768,768]{2,1,0:T(8,128)(2,1)} %s_ref.1, bf16[2,192,768]{2,1,0:T(8,128)(2,1)} %bitcast.5, ...), custom_call_target="tpu_custom_call" | custom-call | tf_op jit(solution)/shard_map/prepare/pallas_call | solution.py:347
  7.0 3.0 %collective-permute-start = (bf16[2,64,256]{2,1,0:T(8,128)(2,1)}, bf16[2,64,256]{2,1,0:T(8,128)(2,1)S(1)}, u32[]{:S(2)}, u32[]{:S(2)}) collective-permute-start(bf16[2,64,256]{2,1,0:T(8,128)(2,1)} %get-tuple-element.13), channel_id=1, source_target_pairs={{0,1},{1,0},{2,3},{3,2},{4,5},{5,4},{6,7},{7,6},{8,9},{9,8},{10,11... | collective-permute-start | bytes 196616 | tf_op jit(solution)/shard_map/ppermute | solution.py:67
  10.0 2.5 %collective-permute-done = bf16[2,64,256]{2,1,0:T(8,128)(2,1)S(1)} collective-permute-done((bf16[2,64,256]{2,1,0:T(8,128)(2,1)}, bf16[2,64,256]{2,1,0:T(8,128)(2,1)S(1)}, u32[]{:S(2)}, u32[]{:S(2)}) %collective-permute-start) | collective-permute-done | bytes 65568 | tf_op jit(solution)/shard_map/ppermute | solution.py:67
  12.4 0.9 %pad_maximum_fusion.refs_0_ = bf16[2,2,64,256]{3,2,1,0:T(8,128)(2,1)S(1)} fusion(bf16[1,2,64,256]{3,2,1,0:T(8,128)(2,1)S(1)} %bitcast.7, bf16[1,2,64,256]{3,2,1,0:T(8,128)(2,1)} %bitcast.6), kind=kLoop, calls=%fused_computation | loop fusion | flops 65536 | bytes 262144 | tf_op jit(solution)/shard_map/stack | solution.py:68
  13.3 0.0 copy-start
  13.3 4.2 %collective-permute-start.3 = (bf16[2,2,64,256]{3,2,1,0:T(8,128)(2,1)S(1)}, bf16[2,2,64,256]{3,2,1,0:T(8,128)(2,1)S(1)}, u32[]{:S(2)}, u32[]{:S(2)}) collective-permute-start(bf16[2,2,64,256]{3,2,1,0:T(8,128)(2,1)S(1)} %pad_maximum_fusion.refs_0_), channel_id=1, source_target_pairs={{0,6},{1,7},{2,0},{3,1},{4,2},{5,3},{6,4},{7,5},{8,14},{9,15},{10,... | collective-permute-start | bytes 393224 | tf_op jit(solution)/shard_map/ppermute | solution.py:70
  17.5 0.0 collective-permute-start.2
  17.5 1.0 %collective-permute-start.1 = (bf16[2,2,64,256]{3,2,1,0:T(8,128)(2,1)S(1)}, bf16[2,2,64,256]{3,2,1,0:T(8,128)(2,1)S(1)}, u32[]{:S(2)}, u32[]{:S(2)}) collective-permute-start(bf16[2,2,64,256]{3,2,1,0:T(8,128)(2,1)S(1)} %pad_maximum_fusion.refs_0_), channel_id=1, source_target_pairs={{0,2},{1,3},{2,4},{3,5},{4,6},{5,7},{6,0},{7,1},{8,10},{9,11},{10,... | collective-permute-start | bytes 393224 | tf_op jit(solution)/shard_map/ppermute | solution.py:70
  18.5 2.9 %collective-permute-done.3.refs_3_ = bf16[2,2,64,256]{3,2,1,0:T(8,128)(2,1)S(1)} collective-permute-done((bf16[2,2,64,256]{3,2,1,0:T(8,128)(2,1)S(1)}, bf16[2,2,64,256]{3,2,1,0:T(8,128)(2,1)S(1)}, u32[]{:S(2)}, u32[]{:S(2)}) %collective-permute-start.3) | collective-permute-done | bytes 131104 | tf_op jit(solution)/shard_map/ppermute | solution.py:70
  21.4 0.0 copy-start.1
  21.4 6.9 %collective-permute-done.2.refs_2_ = bf16[2,2,64,256]{3,2,1,0:T(8,128)(2,1)S(1)} collective-permute-done((bf16[2,2,64,256]{3,2,1,0:T(8,128)(2,1)S(1)}, bf16[2,2,64,256]{3,2,1,0:T(8,128)(2,1)S(1)}, u32[]{:S(2)}, u32[]{:S(2)}) %collective-permute-start.2) | collective-permute-done | bytes 131104 | tf_op jit(solution)/shard_map/ppermute | solution.py:70
  28.3 0.0 copy-start.2
  28.3 0.0 collective-permute-done.1.refs_1_
  28.3 0.0 copy-start.3
  28.3 0.0 copy-done
  28.3 0.0 copy-done.1
  28.3 0.6 %copy-done.2 = bf16[2,2,64,256]{3,2,1,0:T(8,128)(2,1)} copy-done((bf16[2,2,64,256]{3,2,1,0:T(8,128)(2,1)}, bf16[2,2,64,256]{3,2,1,0:T(8,128)(2,1)S(1)}, u32[]{:S(2)}) %copy-start.2) | copy-done | bytes 131096
  29.0 0.0 copy-done.3
  29.0 7.8 %iterate.1 = (bf16[480,128]{1,0:T(8,128)(2,1)}, f32[2,64,192]{2,1,0:T(8,128)}, f32[2,64,192]{2,1,0:T(8,128)}, bf16[2,64,128]{2,1,0:T(8,128)(2,1)}, bf16[2,64,128...) custom-call(s32[1]{0:T(128)} %bitcast.my_ref, bf16[2,2,64,256]{3,2,1,0:T(8,128)(2,1)} %copy-done, ...), custom_call_target="tpu_custom_call" | custom-call | tf_op jit(solution)/shard_map/iterate/pallas_call | solution.py:393
  36.8 0.1 collective-permute-start.6
  36.9 1.5 %collective-permute-start.5 = (bf16[480,128]{1,0:T(8,128)(2,1)}, bf16[480,128]{1,0:T(8,128)(2,1)S(1)}, u32[]{:S(2)}, u32[]{:S(2)}) collective-permute-start(bf16[480,128]{1,0:T(8,128)(2,1)} %get-tuple-element.15.refs_0_), channel_id=1, source_target_pairs={{0,16},{8,24},{16,0},{24,8},{1,17},{9,25},{17,1},{25,9},{2,18},{10... | collective-permute-start | bytes 368648 | tf_op jit(solution)/shard_map/ppermute | solution.py:91
  38.3 0.3 collective-permute-start.4
  38.7 3.9 %collective-permute-done.6.refs_3_ = bf16[480,128]{1,0:T(8,128)(2,1)S(1)} collective-permute-done((bf16[480,128]{1,0:T(8,128)(2,1)}, bf16[480,128]{1,0:T(8,128)(2,1)S(1)}, u32[]{:S(2)}, u32[]{:S(2)}) %collective-permute-start.6) | collective-permute-done | bytes 122912 | tf_op jit(solution)/shard_map/ppermute | solution.py:91
  42.6 0.0 copy-start.4
  42.6 2.7 %collective-permute-done.5.refs_2_ = bf16[480,128]{1,0:T(8,128)(2,1)S(1)} collective-permute-done((bf16[480,128]{1,0:T(8,128)(2,1)}, bf16[480,128]{1,0:T(8,128)(2,1)S(1)}, u32[]{:S(2)}, u32[]{:S(2)}) %collective-permute-start.5) | collective-permute-done | bytes 122912 | tf_op jit(solution)/shard_map/ppermute | solution.py:91
  45.3 0.0 copy-start.5
  45.3 0.0 collective-permute-done.4.refs_1_
  45.3 0.0 copy-start.6
  45.3 0.0 copy-done.4
  45.3 0.6 %copy-done.5 = bf16[480,128]{1,0:T(8,128)(2,1)} copy-done((bf16[480,128]{1,0:T(8,128)(2,1)}, bf16[480,128]{1,0:T(8,128)(2,1)S(1)}, u32[]{:S(2)}) %copy-start.5) | copy-done | bytes 122904
  45.9 0.0 copy-done.6
  46.0 3.4 %finish.1 = (f32[2,64,768]{2,1,0:T(8,128)}, f32[2,64,192]{2,1,0:T(8,128)}, f32[16,48]{1,0:T(8,128)}) custom-call(bf16[480,128]{1,0:T(8,128)(2,1)} %get-tuple-element.15.refs_0_, bf16[480,128]{1,0:T(8,128)(2,1)} %copy-done.6, bf16[480,128]{1,0:T(8,128)(2,1)} %copy-done.5, bf16[480,128]{1,0:T(8,128)(2,1)} %copy-done.4, f32[16,48]{1,0:T(8,128)} %refs_4_.3, ...), custom_call_target="tpu_custom_call" | custom-call | tf_op jit(solution)/shard_map/finish/pallas_call | solution.py:425
Async XLA Ops:
  7.0 5.5 %collective-permute-start = (bf16[2,64,256]{2,1,0:T(8,128)(2,1)}, bf16[2,64,256]{2,1,0:T(8,128)(2,1)S(1)}, u32[]{:S(2)}, u32[]{:S(2)}) collective-permute-start(bf16[2,64,256]{2,1,0:T(8,128)(2,1)} %get-tuple-element.13), channel_id=1, source_target_pairs={{0,1},{1,0},{2,3},{3,2},{4,5},{5,4},{6,7},{7,6},{8,9},{9,8},{10,11... | collective-permute-start | bytes 196616 | tf_op jit(solution)/shard_map/ppermute | solution.py:67
  13.3 15.0 %copy-start = (bf16[2,2,64,256]{3,2,1,0:T(8,128)(2,1)}, bf16[2,2,64,256]{3,2,1,0:T(8,128)(2,1)S(1)}, u32[]{:S(2)}) copy-start(bf16[2,2,64,256]{3,2,1,0:T(8,128)(2,1)S(1)} %pad_maximum_fusion.refs_0_) | copy-start | bytes 393220
  13.3 8.1 %collective-permute-start.3 = (bf16[2,2,64,256]{3,2,1,0:T(8,128)(2,1)S(1)}, bf16[2,2,64,256]{3,2,1,0:T(8,128)(2,1)S(1)}, u32[]{:S(2)}, u32[]{:S(2)}) collective-permute-start(bf16[2,2,64,256]{3,2,1,0:T(8,128)(2,1)S(1)} %pad_maximum_fusion.refs_0_), channel_id=1, source_target_pairs={{0,6},{1,7},{2,0},{3,1},{4,2},{5,3},{6,4},{7,5},{8,14},{9,15},{10,... | collective-permute-start | bytes 393224 | tf_op jit(solution)/shard_map/ppermute | solution.py:70
  17.5 10.8 %collective-permute-start.2 = (bf16[2,2,64,256]{3,2,1,0:T(8,128)(2,1)S(1)}, bf16[2,2,64,256]{3,2,1,0:T(8,128)(2,1)S(1)}, u32[]{:S(2)}, u32[]{:S(2)}) collective-permute-start(bf16[2,2,64,256]{3,2,1,0:T(8,128)(2,1)S(1)} %pad_maximum_fusion.refs_0_), channel_id=1, source_target_pairs={{0,4},{1,5},{2,6},{3,7},{4,0},{5,1},{6,2},{7,3},{8,12},{9,13},{10,... | collective-permute-start | bytes 393224 | tf_op jit(solution)/shard_map/ppermute | solution.py:70
  17.5 10.8 %collective-permute-start.1 = (bf16[2,2,64,256]{3,2,1,0:T(8,128)(2,1)S(1)}, bf16[2,2,64,256]{3,2,1,0:T(8,128)(2,1)S(1)}, u32[]{:S(2)}, u32[]{:S(2)}) collective-permute-start(bf16[2,2,64,256]{3,2,1,0:T(8,128)(2,1)S(1)} %pad_maximum_fusion.refs_0_), channel_id=1, source_target_pairs={{0,2},{1,3},{2,4},{3,5},{4,6},{5,7},{6,0},{7,1},{8,10},{9,11},{10,... | collective-permute-start | bytes 393224 | tf_op jit(solution)/shard_map/ppermute | solution.py:70
  21.4 6.9 %copy-start.1 = (bf16[2,2,64,256]{3,2,1,0:T(8,128)(2,1)}, bf16[2,2,64,256]{3,2,1,0:T(8,128)(2,1)S(1)}, u32[]{:S(2)}) copy-start(bf16[2,2,64,256]{3,2,1,0:T(8,128)(2,1)S(1)} %collective-permute-done.3.refs_3_) | copy-start | bytes 393220
  28.3 0.7 %copy-start.2 = (bf16[2,2,64,256]{3,2,1,0:T(8,128)(2,1)}, bf16[2,2,64,256]{3,2,1,0:T(8,128)(2,1)S(1)}, u32[]{:S(2)}) copy-start(bf16[2,2,64,256]{3,2,1,0:T(8,128)(2,1)S(1)} %collective-permute-done.2.refs_2_) | copy-start | bytes 393220
  28.3 0.7 %copy-start.3 = (bf16[2,2,64,256]{3,2,1,0:T(8,128)(2,1)}, bf16[2,2,64,256]{3,2,1,0:T(8,128)(2,1)S(1)}, u32[]{:S(2)}) copy-start(bf16[2,2,64,256]{3,2,1,0:T(8,128)(2,1)S(1)} %collective-permute-done.1.refs_1_) | copy-start | bytes 393220
  36.8 5.8 %collective-permute-start.6 = (bf16[480,128]{1,0:T(8,128)(2,1)}, bf16[480,128]{1,0:T(8,128)(2,1)S(1)}, u32[]{:S(2)}, u32[]{:S(2)}) collective-permute-start(bf16[480,128]{1,0:T(8,128)(2,1)} %get-tuple-element.15.refs_0_), channel_id=1, source_target_pairs={{0,24},{8,16},{16,8},{24,0},{1,25},{9,17},{17,9},{25,1},{2,26},{10... | collective-permute-start | bytes 368648 | tf_op jit(solution)/shard_map/ppermute | solution.py:91
  36.9 8.4 %collective-permute-start.5 = (bf16[480,128]{1,0:T(8,128)(2,1)}, bf16[480,128]{1,0:T(8,128)(2,1)S(1)}, u32[]{:S(2)}, u32[]{:S(2)}) collective-permute-start(bf16[480,128]{1,0:T(8,128)(2,1)} %get-tuple-element.15.refs_0_), channel_id=1, source_target_pairs={{0,16},{8,24},{16,0},{24,8},{1,17},{9,25},{17,1},{25,9},{2,18},{10... | collective-permute-start | bytes 368648 | tf_op jit(solution)/shard_map/ppermute | solution.py:91
  38.3 6.9 %collective-permute-start.4 = (bf16[480,128]{1,0:T(8,128)(2,1)}, bf16[480,128]{1,0:T(8,128)(2,1)S(1)}, u32[]{:S(2)}, u32[]{:S(2)}) collective-permute-start(bf16[480,128]{1,0:T(8,128)(2,1)} %get-tuple-element.15.refs_0_), channel_id=1, source_target_pairs={{0,8},{8,0},{16,24},{24,16},{1,9},{9,1},{17,25},{25,17},{2,10},{10... | collective-permute-start | bytes 368648 | tf_op jit(solution)/shard_map/ppermute | solution.py:91
  42.6 2.7 %copy-start.4 = (bf16[480,128]{1,0:T(8,128)(2,1)}, bf16[480,128]{1,0:T(8,128)(2,1)S(1)}, u32[]{:S(2)}) copy-start(bf16[480,128]{1,0:T(8,128)(2,1)S(1)} %collective-permute-done.6.refs_3_) | copy-start | bytes 368644
  45.3 0.7 %copy-start.5 = (bf16[480,128]{1,0:T(8,128)(2,1)}, bf16[480,128]{1,0:T(8,128)(2,1)S(1)}, u32[]{:S(2)}) copy-start(bf16[480,128]{1,0:T(8,128)(2,1)S(1)} %collective-permute-done.5.refs_2_) | copy-start | bytes 368644
  45.3 0.7 %copy-start.6 = (bf16[480,128]{1,0:T(8,128)(2,1)}, bf16[480,128]{1,0:T(8,128)(2,1)S(1)}, u32[]{:S(2)}) copy-start(bf16[480,128]{1,0:T(8,128)(2,1)S(1)} %collective-permute-done.4.refs_1_) | copy-start | bytes 368644
